TPU v7x, 256 devices: a whole 4x4x8 slice. The times are simulated.
256 devices in a mesh: pipe: 4 (over y), expert: 16 (over z, core), dp: 4 (over x).
Axes of the slice: x: 4, y: 4, z: 8, core: 2. Of those that a mesh axis runs over, the one named last changes fastest.
Arguments:
- normed: bfloat16 [4, 4, 3072, 4096], P('pipe', None, ('expert', 'dp')), may hold values from -1.5 to 1.5
- saved_out: bfloat16 [4, 4, 3072, 2, 4096], P('pipe', None, ('expert', 'dp')), may hold values from -0.59765625 to 0.59765625
- expert_grads: bfloat16 [4, 4, 4, 16, 16, 9, 4096], P('pipe', None, 'dp', 'expert'), may hold values from -24 to 24
- routes: int32 [4, 4, 3072, 2], P('pipe', None, ('expert', 'dp')), may hold values from 0 to 15, all different within a row; in each aligned block of 48 rows (0 to 47, 48 to 95, ..., all dimensions but the last counted through in order) at most 9 rows name the same one
- router_weight: bfloat16 [4, 4096, 16], P('pipe'), may hold values from -0.375 to 0.375
- upstream: bfloat16 [4, 3072, 4096], P(None, ('expert', 'dp')), may hold values from -6 to 6
Outputs:
- grad_input: bfloat16 [4, 4, 3072, 4096], P('pipe', None, ('expert', 'dp'))
- router_grad: float32 [4, 4096, 16], P('pipe')
Inputs may be any that keep to these rules, and one draw needn't show every extreme that they name: `routes`: the two experts of a row differ. Within the 48 rows of one device for one section and micro-batch no expert is named more than 9 times, a bound that some expert reaches in some of these blocks.
All inputs are finite; a program needn't handle non-finite values.
Results may differ from a plain program's by a relative error of at most 0.007.
Values may be sent and summed in bfloat16 or wider, within the bound.
No kernel may reach another device: no remote copies, remote signals or barrier semaphores. Data moves between devices by JAX's collectives and lax.ppermute only.
A program may use at most 128 MiB of HBM per device.

v0:
```python
import jax
import jax.numpy as jnp
from jax import lax
from jax.sharding import PartitionSpec as P


def shifted(block, axis, distance):
    devices = range(lax.axis_size(axis))
    route = [(i - distance, i) for i in devices if i - distance in devices]
    return lax.ppermute(block, axis, route)


def slot_index(flat, experts, capacity):
    onehot = (flat[..., None] == jnp.arange(experts, dtype=jnp.int32)).astype(jnp.int32)
    before = jnp.cumsum(onehot, axis=-2) - onehot
    position = jnp.sum(before * onehot, axis=-1)
    return flat * capacity + position


def block_grad(incoming, normed_rows, saved_rows, route_rows, returned, index_rows, router_w):
    experts = router_w.shape[1]
    rows_dev = normed_rows.shape[0]
    width = normed_rows.shape[1]
    logits = jnp.dot(normed_rows, router_w, preferred_element_type=jnp.float32)
    expl = jnp.exp(logits)
    probs = expl / jnp.sum(expl, axis=-1, keepdims=True)
    chosen = (route_rows[..., None] == jnp.arange(experts, dtype=jnp.int32)).astype(jnp.float32)
    gates = jnp.einsum("tke,te->tk", chosen, probs)
    dot_grads = jnp.einsum("td,tkd->tk", incoming, saved_rows, preferred_element_type=jnp.float32)
    weighted = dot_grads * gates
    dense_f = (
        jnp.einsum("tke,tk->te", chosen, weighted) - probs * jnp.sum(weighted, axis=-1)[:, None]
    )
    dense = dense_f.astype(jnp.bfloat16)
    router_term = lax.dot_general(
        dense, router_w, (((1,), (1,)), ((), ())), preferred_element_type=jnp.float32
    )
    back_rows = returned[index_rows].reshape(rows_dev, 2, width).astype(jnp.float32)
    total = (
        incoming.astype(jnp.float32)
        + gates[:, 0, None] * back_rows[:, 0]
        + gates[:, 1, None] * back_rows[:, 1]
        + router_term
    )
    weight_part = lax.dot_general(
        normed_rows, dense, (((0,), (0,)), ((), ())), preferred_element_type=jnp.float32
    )
    return (total.astype(jnp.bfloat16), weight_part)


def on_device(normed, saved_out, expert_grads, routes, router_weight, upstream):
    micro = normed.shape[1]
    rows_dev = normed.shape[2]
    width = normed.shape[3]
    sections = lax.axis_size("pipe")
    section_idx = lax.axis_index("pipe")
    router_w = router_weight[0]
    experts = router_w.shape[1]
    capacity = expert_grads.shape[5]
    slot_rows = slot_index(routes[0].reshape(micro, -1), experts, capacity)
    local_grads = expert_grads[0, :, 0]
    returned_list = []
    for block_num in range(micro):
        received = lax.all_to_all(
            local_grads[block_num], "expert", split_axis=1, concat_axis=0, tiled=True
        )
        returned_list.append(received.reshape(experts * capacity, width))
    returned_all = jnp.stack(returned_list)
    grad_buffer = jnp.zeros((micro, rows_dev, width), jnp.bfloat16)
    weight_sum = jnp.zeros((width, experts), jnp.float32)
    passed = jnp.zeros((rows_dev, width), jnp.bfloat16)
    for tick_num in range(micro + sections - 1):
        if tick_num > 0:
            passed = shifted(passed, "pipe", -1)
        block_num = tick_num - (sections - 1 - section_idx)
        is_active = (block_num >= 0) & (block_num < micro)
        block_idx = jnp.clip(block_num, 0, micro - 1)
        returned = lax.dynamic_index_in_dim(returned_all, block_idx, 0, keepdims=False)
        from_top = lax.dynamic_index_in_dim(upstream, block_idx, 0, keepdims=False)
        incoming = jnp.where(section_idx == sections - 1, from_top, passed)
        new_grad, weight_part = block_grad(
            incoming,
            lax.dynamic_index_in_dim(normed[0], block_idx, 0, keepdims=False),
            lax.dynamic_index_in_dim(saved_out[0], block_idx, 0, keepdims=False),
            lax.dynamic_index_in_dim(routes[0], block_idx, 0, keepdims=False),
            returned,
            lax.dynamic_index_in_dim(slot_rows, block_idx, 0, keepdims=False),
            router_w,
        )
        updated = lax.dynamic_update_index_in_dim(grad_buffer, new_grad, block_idx, 0)
        grad_buffer = jnp.where(is_active, updated, grad_buffer)
        weight_sum = weight_sum + jnp.where(is_active, weight_part, 0.0)
        passed = new_grad
    router_grad = lax.psum(weight_sum / micro, ("expert", "dp"))
    return (grad_buffer[None], router_grad[None])


def solution(mesh):
    in_specs = (
        P("pipe", None, ("expert", "dp"), None),
        P("pipe", None, ("expert", "dp"), None, None),
        P("pipe", None, "dp", "expert", None, None, None),
        P("pipe", None, ("expert", "dp"), None),
        P("pipe", None, None),
        P(None, ("expert", "dp"), None),
    )
    out_specs = (P("pipe", None, ("expert", "dp"), None), P("pipe", None, None))
    return jax.shard_map(
        on_device, mesh=mesh, in_specs=in_specs, out_specs=out_specs, check_vma=False
    )
```

profile of v0, /device:TPU:1, one launch (start us, length us, event | category | flops | bytes accessed | tf_op | source)
XLA Modules:
  0.0 636.1 jit_solution(2353032965511129839)
XLA Ops:
  7.2 4.4 fusion.196
  13.7 10.1 %all-to-all-start = ((bf16[1,16,9,4096]{3,2,0,1:T(8,128)(2,1)}), bf16[1,16,9,4096]{3,2,0,1:T(8,128)(2,1)}, u32[]{:S(2)}, u32[]{:S(2)}) async-start(bf16[1,16,9,4096]{3,2,0,1:T(8,128)(2,1)} %bitcast.551), calls=%async_computation | async-start | bytes 4194304 | tf_op jit(solution)/shard_map/all_to_all | solution.py:64
  30.8 3.4 copy.366
  39.4 33.5 %all-to-all-done = bf16[1,16,9,4096]{3,2,0,1:T(8,128)(2,1)} async-done(((bf16[1,16,9,4096]{3,2,0,1:T(8,128)(2,1)}), bf16[1,16,9,4096]{3,2,0,1:T(8,128)(2,1)}, u32[]{:S(2)}, u32[]{:S(2)}) %all-to-all-start) | async-done | bytes 1179680 | tf_op jit(solution)/shard_map/all_to_all | solution.py:64
  72.9 5.0 all-to-all-start.1
  78.8 3.5 copy.365
  97.5 29.4 %all-to-all-done.1 = bf16[1,16,9,4096]{3,2,0,1:T(8,128)(2,1)} async-done(((bf16[1,16,9,4096]{3,2,0,1:T(8,128)(2,1)}), bf16[1,16,9,4096]{3,2,0,1:T(8,128)(2,1)}, u32[]{:S(2)}, u32[]{:S(2)}) %all-to-all-start.1) | async-done | bytes 1179680 | tf_op jit(solution)/shard_map/all_to_all | solution.py:64
  126.9 5.0 all-to-all-start.2
  143.3 37.7 %all-to-all-done.2 = bf16[1,16,9,4096]{3,2,0,1:T(8,128)(2,1)} async-done(((bf16[1,16,9,4096]{3,2,0,1:T(8,128)(2,1)}), bf16[1,16,9,4096]{3,2,0,1:T(8,128)(2,1)}, u32[]{:S(2)}, u32[]{:S(2)}) %all-to-all-start.2) | async-done | bytes 1179680 | tf_op jit(solution)/shard_map/all_to_all | solution.py:64
  181.0 5.1 all-to-all-start.3
  201.4 33.7 %all-to-all-done.3 = bf16[1,16,9,4096]{3,2,0,1:T(8,128)(2,1)} async-done(((bf16[1,16,9,4096]{3,2,0,1:T(8,128)(2,1)}), bf16[1,16,9,4096]{3,2,0,1:T(8,128)(2,1)}, u32[]{:S(2)}, u32[]{:S(2)}) %all-to-all-start.3) | async-done | bytes 1179680 | tf_op jit(solution)/shard_map/all_to_all | solution.py:64
  240.2 7.0 %dynamic-slice_bitcast_fusion = (bf16[144,4096]{1,0:T(8,128)(2,1)}, bf16[144,4096]{1,0:T(8,128)(2,1)}, bf16[144,4096]{1,0:T(8,128)(2,1)}, bf16[144,4096]{1,0:T(8...) fusion(bf16[4,144,4096]{2,1,0:T(8,128)(2,1)} %constant_dynamic-update-slice_fusion, ...), kind=kLoop, calls=%fused_computation.28 | loop fusion | bytes 16515100 | tf_op jit(solution)/shard_map/jit(dynamic_index_in_dim)/squeeze | solution.py:78
  247.1 4.1 gather_fusion
  251.3 2.9 reshape.322
  254.2 3.6 fusion.203
  259.1 3.0 bitcast_dynamic-update-slice_fusion
  263.8 4.2 gather_fusion.1
  268.0 2.9 reshape.323
  271.0 4.7 fusion.202
  275.7 4.2 gather_fusion.2
  279.9 2.9 reshape.324
  282.9 4.7 fusion.201
  287.6 4.2 gather_fusion.3
  291.8 3.1 reshape.325
  294.9 4.7 fusion.200
  299.6 4.3 gather_fusion.4
  303.9 2.9 reshape.326
  308.0 2.7 fusion.50
  319.0 3.8 fusion.81
  324.1 3.0 fusion.199
  327.1 4.2 gather_fusion.5
  331.3 3.1 reshape.327
  337.2 2.7 fusion.51
  348.2 3.8 fusion.78
  353.2 2.9 fusion.198
  356.2 4.3 gather_fusion.6
  360.5 2.9 reshape.328
  364.8 2.7 fusion.52
  375.8 3.6 fusion.75
  381.1 2.9 fusion.197
  385.9 4.9 collective-permute-done.3
  395.4 3.7 fusion.72
  400.8 8.6 %collective-permute-done.4 = bf16[48,4096]{1,0:T(8,128)(2,1)S(1)} collective-permute-done((bf16[48,4096]{1,0:T(8,128)(2,1)S(1)}, bf16[48,4096]{1,0:T(8,128)(2,1)S(1)}, u32[]{:S(2)}, u32[]{:S(2)}) %collective-permute-start.4) | collective-permute-done | bytes 393248 | tf_op jit(solution)/shard_map/ppermute | solution.py:10
  411.2 2.7 fusion.54
  421.9 3.6 fusion.69
  430.0 4.8 collective-permute-done.5
  449.5 3.5 fusion.66
  453.1 174.1 %all-reduce.2.cloned.1.call-done = f32[1,4096,16]{1,2,0:T(8,128)} async-done(((f32[1,4096,16]{1,2,0:T(8,128)}), f32[1,4096,16]{1,2,0:T(8,128)}) %all-reduce.2.cloned.1.call-update) | async-done | bytes 262160 | tf_op jit(solution)/shard_map/psum | solution.py:94
  (270 shorter events, 137.6 us)
Async XLA Ops:
  7.2 20.7 %copy-start = (bf16[1,4,48,2,4096]{4,3,2,1,0:T(2,128)(2,1)S(1)}, bf16[1,4,48,2,4096]{4,3,2,1,0:T(2,128)(2,1)}, u32[]{:S(2)}) copy-start(bf16[1,4,48,2,4096]{4,3,2,1,0:T(2,128)(2,1)} %param.7) | copy-start | bytes 9437188
  13.7 10.1 %copy-start.43 = (s32[1,4,48,2]{2,3,1,0:T(2,128)S(1)}, s32[1,4,48,2]{2,3,1,0:T(2,128)}, u32[]{:S(2)}) copy-start(s32[1,4,48,2]{2,3,1,0:T(2,128)} %param.9) | copy-start | bytes 4612
  13.7 10.9 %copy-start.1 = (bf16[1,4096,16]{1,2,0:T(8,128)(2,1)S(1)}, bf16[1,4096,16]{1,2,0:T(8,128)(2,1)}, u32[]{:S(2)}) copy-start(bf16[1,4096,16]{1,2,0:T(8,128)(2,1)} %param.10) | copy-start | bytes 393220
  13.7 59.2 %all-to-all-start = ((bf16[1,16,9,4096]{3,2,0,1:T(8,128)(2,1)}), bf16[1,16,9,4096]{3,2,0,1:T(8,128)(2,1)}, u32[]{:S(2)}, u32[]{:S(2)}) async-start(bf16[1,16,9,4096]{3,2,0,1:T(8,128)(2,1)} %bitcast.551), calls=%async_computation | async-start | bytes 4194304 | tf_op jit(solution)/shard_map/all_to_all | solution.py:64
  26.8 3.3 copy-start.47
  34.2 38.7 %copy-start.41 = (s32[4,96]{1,0:T(4,128)}, s32[4,96]{1,0:T(4,128)S(1)}, u32[]{:S(2)}) copy-start(s32[4,96]{1,0:T(4,128)S(1)} %copy.75) | copy-start | bytes 4612
  34.3 38.6 %copy-start.20 = (s32[48,2]{1,0:T(8,128)}, s32[48,2]{1,0:T(8,128)S(1)}, u32[]{:S(2)}) copy-start(s32[48,2]{1,0:T(8,128)S(1)} %copy.79) | copy-start | bytes 1156
  36.2 41.6 %copy-start.18 = (s32[48,2]{1,0:T(8,128)}, s32[48,2]{1,0:T(8,128)S(1)}, u32[]{:S(2)}) copy-start(s32[48,2]{1,0:T(8,128)S(1)} %copy.82) | copy-start | bytes 1156
  72.9 54.0 %all-to-all-start.1 = ((bf16[1,16,9,4096]{3,2,0,1:T(8,128)(2,1)}), bf16[1,16,9,4096]{3,2,0,1:T(8,128)(2,1)}, u32[]{:S(2)}, u32[]{:S(2)}) async-start(bf16[1,16,9,4096]{3,2,0,1:T(8,128)(2,1)} %bitcast.550), calls=%async_computation.1 | async-start | bytes 4194304 | tf_op jit(solution)/shard_map/all_to_all | solution.py:64
  78.8 3.5 copy-start.7
  86.9 2.8 copy-start.19
  93.3 2.7 copy-start.15
  96.2 35.7 %copy-start.14 = (s32[48,2]{1,0:T(8,128)}, s32[48,2]{1,0:T(8,128)S(1)}, u32[]{:S(2)}) copy-start(s32[48,2]{1,0:T(8,128)S(1)} %copy.94) | copy-start | bytes 1156
  97.4 29.5 %copy-start.48 = (f32[48]{0:T(128)}, f32[48]{0:T(128)S(1)}, u32[]{:S(2)}) copy-start(f32[48]{0:T(128)S(1)} %get-tuple-element.93) | copy-start | bytes 580
  126.9 54.0 %all-to-all-start.2 = ((bf16[1,16,9,4096]{3,2,0,1:T(8,128)(2,1)}), bf16[1,16,9,4096]{3,2,0,1:T(8,128)(2,1)}, u32[]{:S(2)}, u32[]{:S(2)}) async-start(bf16[1,16,9,4096]{3,2,0,1:T(8,128)(2,1)} %bitcast.549), calls=%async_computation.2 | async-start | bytes 4194304 | tf_op jit(solution)/shard_map/all_to_all | solution.py:64
  132.2 54.2 %copy-start.44 = (f32[48,2]{0,1:T(2,128)}, f32[48,2]{0,1:T(2,128)S(1)}, u32[]{:S(2)}) copy-start(f32[48,2]{0,1:T(2,128)S(1)} %copy.167) | copy-start | bytes 1156
  180.9 6.0 copy-start.32
  181.0 6.0 copy-start.42
  181.0 6.0 copy-start.57
  181.0 6.0 copy-start.60
  181.0 54.2 %all-to-all-start.3 = ((bf16[1,16,9,4096]{3,2,0,1:T(8,128)(2,1)}), bf16[1,16,9,4096]{3,2,0,1:T(8,128)(2,1)}, u32[]{:S(2)}, u32[]{:S(2)}) async-start(bf16[1,16,9,4096]{3,2,0,1:T(8,128)(2,1)} %bitcast.548), calls=%async_computation.3 | async-start | bytes 4194304 | tf_op jit(solution)/shard_map/all_to_all | solution.py:64
  186.1 441.1 %all-reduce.2.cloned.1.call-start = ((), (), s32[]{:S(2)}) async-start(), calls=%async_computation.4 | async-start | bytes 524288 | tf_op jit(solution)/shard_map/psum | solution.py:94
  262.1 44.7 %collective-permute-start = (bf16[48,4096]{1,0:T(8,128)(2,1)}, bf16[48,4096]{1,0:T(8,128)(2,1)}, u32[]{:S(2)}, u32[]{:S(2)}) collective-permute-start(bf16[48,4096]{1,0:T(8,128)(2,1)} %get-tuple-element.72), channel_id=1, source_target_pairs={{64,0},{128,64},{192,128},{65,1},{129,65},{193,129},{66,2},{130,66... | collective-permute-start | bytes 1179656 | tf_op jit(solution)/shard_map/ppermute | solution.py:10
  308.0 10.3 %copy-start.30 = (f32[48,16]{0,1:T(8,128)S(1)}, f32[48,16]{0,1:T(8,128)}, u32[]{:S(2)}) copy-start(f32[48,16]{0,1:T(8,128)} %copy-done.29) | copy-start | bytes 9220
  319.0 3.8 copy-start.33
  319.0 5.1 copy-start.4
  322.8 13.2 %collective-permute-start.1 = (bf16[48,4096]{1,0:T(8,128)(2,1)}, bf16[48,4096]{1,0:T(8,128)(2,1)}, u32[]{:S(2)}, u32[]{:S(2)}) collective-permute-start(bf16[48,4096]{1,0:T(8,128)(2,1)} %get-tuple-element.76), channel_id=1, source_target_pairs={{64,0},{128,64},{192,128},{65,1},{129,65},{193,129},{66,2},{130,66... | collective-permute-start | bytes 1179656 | tf_op jit(solution)/shard_map/ppermute | solution.py:10
  337.1 10.3 %copy-start.26 = (f32[48,16]{0,1:T(8,128)S(1)}, f32[48,16]{0,1:T(8,128)}, u32[]{:S(2)}) copy-start(f32[48,16]{0,1:T(8,128)} %copy-done.25) | copy-start | bytes 9220
  348.2 3.8 copy-start.35
  348.2 5.1 copy-start.5
  352.0 11.6 %collective-permute-start.2 = (bf16[48,4096]{1,0:T(8,128)(2,1)}, bf16[48,4096]{1,0:T(8,128)(2,1)}, u32[]{:S(2)}, u32[]{:S(2)}) collective-permute-start(bf16[48,4096]{1,0:T(8,128)(2,1)} %get-tuple-element.80), channel_id=1, source_target_pairs={{64,0},{128,64},{192,128},{65,1},{129,65},{193,129},{66,2},{130,66... | collective-permute-start | bytes 1179656 | tf_op jit(solution)/shard_map/ppermute | solution.py:10
  364.7 10.3 %copy-start.28 = (f32[48,16]{0,1:T(8,128)S(1)}, f32[48,16]{0,1:T(8,128)}, u32[]{:S(2)}) copy-start(f32[48,16]{0,1:T(8,128)} %copy-done.27) | copy-start | bytes 9220
  375.8 3.7 copy-start.37
  375.8 5.3 copy-start.6
  379.4 4.6 copy-start.34
  379.4 11.4 %collective-permute-start.3 = (bf16[48,4096]{1,0:T(8,128)(2,1)S(1)}, bf16[48,4096]{1,0:T(8,128)(2,1)S(1)}, u32[]{:S(2)}, u32[]{:S(2)}) collective-permute-start(bf16[48,4096]{1,0:T(8,128)(2,1)S(1)} %get-tuple-element.84), channel_id=1, source_target_pairs={{64,0},{128,64},{192,128},{65,1},{129,65},{193,129},{66,2},{130,66... | collective-permute-start | bytes 1179656 | tf_op jit(solution)/shard_map/ppermute | solution.py:10
  395.3 3.7 copy-start.39
  395.3 5.0 copy-start.2
  395.4 5.0 copy-start.13
  395.4 5.0 copy-start.36
  395.4 5.2 copy-start.38
  399.1 10.3 %collective-permute-start.4 = (bf16[48,4096]{1,0:T(8,128)(2,1)S(1)}, bf16[48,4096]{1,0:T(8,128)(2,1)S(1)}, u32[]{:S(2)}, u32[]{:S(2)}) collective-permute-start(bf16[48,4096]{1,0:T(8,128)(2,1)S(1)} %get-tuple-element.88), channel_id=1, source_target_pairs={{64,0},{128,64},{192,128},{65,1},{129,65},{193,129},{66,2},{130,66... | collective-permute-start | bytes 1179656 | tf_op jit(solution)/shard_map/ppermute | solution.py:10
  411.2 10.1 %copy-start.22 = (f32[48,16]{0,1:T(8,128)S(1)}, f32[48,16]{0,1:T(8,128)}, u32[]{:S(2)}) copy-start(f32[48,16]{0,1:T(8,128)} %copy-done.21) | copy-start | bytes 9220
  421.9 4.9 copy-start.3
  421.9 5.0 copy-start.40
  425.6 9.2 %collective-permute-start.5 = (bf16[48,4096]{1,0:T(8,128)(2,1)S(1)}, bf16[48,4096]{1,0:T(8,128)(2,1)S(1)}, u32[]{:S(2)}, u32[]{:S(2)}) collective-permute-start(bf16[48,4096]{1,0:T(8,128)(2,1)S(1)} %get-tuple-element.92), channel_id=1, source_target_pairs={{64,0},{128,64},{192,128},{65,1},{129,65},{193,129},{66,2},{130,66... | collective-permute-start | bytes 1179656 | tf_op jit(solution)/shard_map/ppermute | solution.py:10
  436.6 4.2 copy-start.45
  436.6 10.3 %copy-start.49 = (f32[48]{0:T(128)S(1)}, f32[48]{0:T(128)}, u32[]{:S(2)}) copy-start(f32[48]{0:T(128)} %copy-done.48) | copy-start | bytes 580
  (26 other events, 34.4 us)
Sparse Core Ops, SparseCore 0:
  449.7 177.4 all-reduce.1
where the time goes:
time: 646 us; the launch traced here: 636 us
  waiting for transfers between devices  328 us (51%)
  local copies, waits for them, and re-layouts  165 us (26%)
  matrix products  57.4 us (9%)
  other arithmetic  35.6 us (6%)
  starting transfers between devices  33.9 us (5%)
  between operations  15.2 us (2%)
    psum x1, waiting for transfers between devices, on_device(): router_grad = lax.psum(weight_sum / micro, ('expert', 'dp'))  174 us
    all_to_all x4, waiting for transfers between devices, on_device(): lax.all_to_all(local_grads[block_num], 'expert', split_axis=1, concat_axi...  134 us
    unnamed x150, local copies, waits for them, and re-layouts  34.3 us
    gather x7, local copies, waits for them, and re-layouts, block_grad(): returned[index_rows].reshape(rows_dev, 2, width).astype(jnp.float32)  29.6 us
    slice x7, local copies, waits for them, and re-layouts, block_grad(): back_rows[:, 0]  26.5 us
    all_to_all x4, starting transfers between devices, on_device(): lax.all_to_all(local_grads[block_num], 'expert', split_axis=1, concat_axi...  25.2 us
    dot_general x7, matrix products, block_grad(): lax.dot_general(dense, router_w, (((1,), (1,)), ((), ())), preferred_elem...  25 us
    convert_element_type x7, local copies, waits for them, and re-layouts, block_grad(): returned[index_rows].reshape(rows_dev, 2, width).astype(jnp.float32)  20.9 us
  transfers between devices with their start and end apart: 11, of which 10 were waited for; matrix products, arithmetic and copies ran while one was open for 21% of the time, Pallas kernels for 0%

commit v1 on v0

--- a/solution.py
+++ b/solution.py
@@ -91,7 +91,7 @@
         grad_buffer = jnp.where(is_active, updated, grad_buffer)
         weight_sum = weight_sum + jnp.where(is_active, weight_part, 0.0)
         passed = new_grad
-    router_grad = lax.psum(weight_sum / micro, ("expert", "dp"))
+    router_grad = lax.psum(lax.psum(weight_sum / micro, "dp"), "expert")
     return (grad_buffer[None], router_grad[None])
 
 

time: 646 us -> 620 us (0.960)
  waiting for transfers between devices: 328 us -> 304 us
    psum x1 -> x2, waiting for transfers between devices: 174 us -> 149 us  [on_device(): router_grad = lax.psum(lax.psum(weight_sum / micro, 'dp'), 'expert')]
    unnamed x150 -> x152, local copies, waits for them, and re-layouts: 34.3 us -> 33.4 us
  transfers between devices with their start and end apart: 11 -> 12, of which waited for: 10 -> 10; matrix products, arithmetic and copies ran while one was open for 21% -> 22% of each run, Pallas kernels for 0% -> 0%
where the time goes in v1:
time: 620 us; the launch traced here: 610 us
  waiting for transfers between devices  304 us (49%)
  local copies, waits for them, and re-layouts  164 us (26%)
  matrix products  57.5 us (9%)
  other arithmetic  35.8 us (6%)
  starting transfers between devices  33.8 us (5%)
  between operations  15.3 us (2%)
    psum x2, waiting for transfers between devices, on_device(): router_grad = lax.psum(lax.psum(weight_sum / micro, 'dp'), 'expert')  149 us
    all_to_all x4, waiting for transfers between devices, on_device(): lax.all_to_all(local_grads[block_num], 'expert', split_axis=1, concat_axi...  134 us
    unnamed x152, local copies, waits for them, and re-layouts  33.4 us
    gather x7, local copies, waits for them, and re-layouts, block_grad(): returned[index_rows].reshape(rows_dev, 2, width).astype(jnp.float32)  29.5 us
    slice x7, local copies, waits for them, and re-layouts, block_grad(): back_rows[:, 0]  26.5 us
    all_to_all x4, starting transfers between devices, on_device(): lax.all_to_all(local_grads[block_num], 'expert', split_axis=1, concat_axi...  25.2 us
    dot_general x7, matrix products, block_grad(): lax.dot_general(dense, router_w, (((1,), (1,)), ((), ())), preferred_elem...  25.1 us
    convert_element_type x7, local copies, waits for them, and re-layouts, block_grad(): returned[index_rows].reshape(rows_dev, 2, width).astype(jnp.float32)  20.9 us
  transfers between devices with their start and end apart: 12, of which 10 were waited for; matrix products, arithmetic and copies ran while one was open for 22% of the time, Pallas kernels for 0%

profile of v1, /device:TPU:1, one launch (start us, length us, event | category | flops | bytes accessed | tf_op | source)
XLA Modules:
  0.0 610.4 jit_solution(6269259830932136821)
XLA Ops:
  7.2 4.4 fusion.195
  13.7 10.1 %all-to-all-start = ((bf16[1,16,9,4096]{3,2,0,1:T(8,128)(2,1)}), bf16[1,16,9,4096]{3,2,0,1:T(8,128)(2,1)}, u32[]{:S(2)}, u32[]{:S(2)}) async-start(bf16[1,16,9,4096]{3,2,0,1:T(8,128)(2,1)} %bitcast.550), calls=%async_computation | async-start | bytes 4194304 | tf_op jit(solution)/shard_map/all_to_all | solution.py:64
  30.7 3.4 copy.366
  39.3 33.5 %all-to-all-done = bf16[1,16,9,4096]{3,2,0,1:T(8,128)(2,1)} async-done(((bf16[1,16,9,4096]{3,2,0,1:T(8,128)(2,1)}), bf16[1,16,9,4096]{3,2,0,1:T(8,128)(2,1)}, u32[]{:S(2)}, u32[]{:S(2)}) %all-to-all-start) | async-done | bytes 1179680 | tf_op jit(solution)/shard_map/all_to_all | solution.py:64
  72.9 5.0 all-to-all-start.1
  78.7 3.5 copy.365
  97.5 29.4 %all-to-all-done.1 = bf16[1,16,9,4096]{3,2,0,1:T(8,128)(2,1)} async-done(((bf16[1,16,9,4096]{3,2,0,1:T(8,128)(2,1)}), bf16[1,16,9,4096]{3,2,0,1:T(8,128)(2,1)}, u32[]{:S(2)}, u32[]{:S(2)}) %all-to-all-start.1) | async-done | bytes 1179680 | tf_op jit(solution)/shard_map/all_to_all | solution.py:64
  126.9 5.0 all-to-all-start.2
  143.5 37.5 %all-to-all-done.2 = bf16[1,16,9,4096]{3,2,0,1:T(8,128)(2,1)} async-done(((bf16[1,16,9,4096]{3,2,0,1:T(8,128)(2,1)}), bf16[1,16,9,4096]{3,2,0,1:T(8,128)(2,1)}, u32[]{:S(2)}, u32[]{:S(2)}) %all-to-all-start.2) | async-done | bytes 1179680 | tf_op jit(solution)/shard_map/all_to_all | solution.py:64
  180.9 5.1 all-to-all-start.3
  201.3 33.8 %all-to-all-done.3 = bf16[1,16,9,4096]{3,2,0,1:T(8,128)(2,1)} async-done(((bf16[1,16,9,4096]{3,2,0,1:T(8,128)(2,1)}), bf16[1,16,9,4096]{3,2,0,1:T(8,128)(2,1)}, u32[]{:S(2)}, u32[]{:S(2)}) %all-to-all-start.3) | async-done | bytes 1179680 | tf_op jit(solution)/shard_map/all_to_all | solution.py:64
  240.1 7.0 %dynamic-slice_bitcast_fusion = (bf16[144,4096]{1,0:T(8,128)(2,1)}, bf16[144,4096]{1,0:T(8,128)(2,1)}, bf16[144,4096]{1,0:T(8,128)(2,1)}, bf16[144,4096]{1,0:T(8...) fusion(bf16[4,144,4096]{2,1,0:T(8,128)(2,1)} %constant_dynamic-update-slice_fusion, ...), kind=kLoop, calls=%fused_computation.27 | loop fusion | bytes 16515100 | tf_op jit(solution)/shard_map/jit(dynamic_index_in_dim)/squeeze | solution.py:78
  247.1 4.1 gather_fusion
  251.2 2.9 reshape.322
  254.2 3.6 fusion.202
  259.1 3.0 bitcast_dynamic-update-slice_fusion
  263.8 4.2 gather_fusion.1
  268.0 2.9 reshape.323
  271.0 4.7 fusion.201
  275.7 4.2 gather_fusion.2
  279.9 2.9 reshape.324
  282.9 4.7 fusion.200
  287.6 4.2 gather_fusion.3
  291.8 3.1 reshape.325
  296.1 2.7 fusion.49
  307.0 3.8 fusion.80
  312.1 3.0 fusion.199
  315.1 4.3 gather_fusion.4
  319.4 2.9 reshape.326
  325.2 2.7 fusion.50
  336.2 3.8 fusion.77
  341.3 2.9 fusion.198
  344.2 4.2 gather_fusion.5
  348.5 3.1 reshape.327
  352.8 2.7 fusion.51
  363.8 3.8 fusion.74
  368.9 3.0 fusion.197
  371.9 4.2 gather_fusion.6
  376.1 2.9 reshape.328
  384.8 3.6 fusion.71
  390.4 10.2 %collective-permute-done.4 = bf16[48,4096]{1,0:T(8,128)(2,1)S(1)} collective-permute-done((bf16[48,4096]{1,0:T(8,128)(2,1)S(1)}, bf16[48,4096]{1,0:T(8,128)(2,1)S(1)}, u32[]{:S(2)}, u32[]{:S(2)}) %collective-permute-start.4) | collective-permute-done | bytes 393248 | tf_op jit(solution)/shard_map/ppermute | solution.py:10
  402.4 2.7 fusion.53
  413.3 3.6 fusion.68
  418.6 8.4 %collective-permute-done.5 = bf16[48,4096]{1,0:T(8,128)(2,1)S(1)} collective-permute-done((bf16[48,4096]{1,0:T(8,128)(2,1)S(1)}, bf16[48,4096]{1,0:T(8,128)(2,1)S(1)}, u32[]{:S(2)}, u32[]{:S(2)}) %collective-permute-start.5) | collective-permute-done | bytes 393248 | tf_op jit(solution)/shard_map/ppermute | solution.py:10
  441.5 4.7 fusion.196
  448.9 39.0 %all-reduce.3.cloned.1.call-done = f32[4096,16]{0,1:T(8,128)} async-done(((f32[4096,16]{0,1:T(8,128)}), f32[4096,16]{0,1:T(8,128)}) %all-reduce.3.cloned.1.call-update) | async-done | bytes 262160 | tf_op jit(solution)/shard_map/psum | solution.py:94
  488.0 3.5 fusion.65
  491.5 109.9 %all-reduce.5.cloned.1.call-done = f32[1,4096,16]{1,2,0:T(8,128)} async-done(((f32[1,4096,16]{1,2,0:T(8,128)}), f32[1,4096,16]{1,2,0:T(8,128)}) %all-reduce.5.cloned.1.call-update) | async-done | bytes 262160 | tf_op jit(solution)/shard_map/psum | solution.py:94
  (275 shorter events, 136.9 us)
Async XLA Ops:
  7.2 20.6 %copy-start = (bf16[1,4,48,2,4096]{4,3,2,1,0:T(2,128)(2,1)S(1)}, bf16[1,4,48,2,4096]{4,3,2,1,0:T(2,128)(2,1)}, u32[]{:S(2)}) copy-start(bf16[1,4,48,2,4096]{4,3,2,1,0:T(2,128)(2,1)} %param.7) | copy-start | bytes 9437188
  13.7 10.1 %copy-start.42 = (s32[1,4,48,2]{2,3,1,0:T(2,128)S(1)}, s32[1,4,48,2]{2,3,1,0:T(2,128)}, u32[]{:S(2)}) copy-start(s32[1,4,48,2]{2,3,1,0:T(2,128)} %param.9) | copy-start | bytes 4612
  13.7 10.9 %copy-start.1 = (bf16[1,4096,16]{1,2,0:T(8,128)(2,1)S(1)}, bf16[1,4096,16]{1,2,0:T(8,128)(2,1)}, u32[]{:S(2)}) copy-start(bf16[1,4096,16]{1,2,0:T(8,128)(2,1)} %param.10) | copy-start | bytes 393220
  13.7 59.2 %all-to-all-start = ((bf16[1,16,9,4096]{3,2,0,1:T(8,128)(2,1)}), bf16[1,16,9,4096]{3,2,0,1:T(8,128)(2,1)}, u32[]{:S(2)}, u32[]{:S(2)}) async-start(bf16[1,16,9,4096]{3,2,0,1:T(8,128)(2,1)} %bitcast.550), calls=%async_computation | async-start | bytes 4194304 | tf_op jit(solution)/shard_map/all_to_all | solution.py:64
  26.8 3.3 copy-start.46
  34.1 38.7 %copy-start.40 = (s32[4,96]{1,0:T(4,128)}, s32[4,96]{1,0:T(4,128)S(1)}, u32[]{:S(2)}) copy-start(s32[4,96]{1,0:T(4,128)S(1)} %copy.75) | copy-start | bytes 4612
  34.2 38.6 %copy-start.19 = (s32[48,2]{1,0:T(8,128)}, s32[48,2]{1,0:T(8,128)S(1)}, u32[]{:S(2)}) copy-start(s32[48,2]{1,0:T(8,128)S(1)} %copy.79) | copy-start | bytes 1156
  36.2 41.6 %copy-start.17 = (s32[48,2]{1,0:T(8,128)}, s32[48,2]{1,0:T(8,128)S(1)}, u32[]{:S(2)}) copy-start(s32[48,2]{1,0:T(8,128)S(1)} %copy.82) | copy-start | bytes 1156
  72.9 54.0 %all-to-all-start.1 = ((bf16[1,16,9,4096]{3,2,0,1:T(8,128)(2,1)}), bf16[1,16,9,4096]{3,2,0,1:T(8,128)(2,1)}, u32[]{:S(2)}, u32[]{:S(2)}) async-start(bf16[1,16,9,4096]{3,2,0,1:T(8,128)(2,1)} %bitcast.549), calls=%async_computation.1 | async-start | bytes 4194304 | tf_op jit(solution)/shard_map/all_to_all | solution.py:64
  78.7 3.5 copy-start.7
  96.2 35.7 %copy-start.13 = (s32[48,2]{1,0:T(8,128)}, s32[48,2]{1,0:T(8,128)S(1)}, u32[]{:S(2)}) copy-start(s32[48,2]{1,0:T(8,128)S(1)} %copy.94) | copy-start | bytes 1156
  97.4 29.5 %copy-start.47 = (f32[48]{0:T(128)}, f32[48]{0:T(128)S(1)}, u32[]{:S(2)}) copy-start(f32[48]{0:T(128)S(1)} %get-tuple-element.93) | copy-start | bytes 580
  126.9 54.0 %all-to-all-start.2 = ((bf16[1,16,9,4096]{3,2,0,1:T(8,128)(2,1)}), bf16[1,16,9,4096]{3,2,0,1:T(8,128)(2,1)}, u32[]{:S(2)}, u32[]{:S(2)}) async-start(bf16[1,16,9,4096]{3,2,0,1:T(8,128)(2,1)} %bitcast.548), calls=%async_computation.2 | async-start | bytes 4194304 | tf_op jit(solution)/shard_map/all_to_all | solution.py:64
  132.2 54.2 %copy-start.43 = (f32[48,2]{0,1:T(2,128)}, f32[48,2]{0,1:T(2,128)S(1)}, u32[]{:S(2)}) copy-start(f32[48,2]{0,1:T(2,128)S(1)} %copy.167) | copy-start | bytes 1156
  180.9 6.0 copy-start.31
  180.9 6.0 copy-start.41
  180.9 6.0 copy-start.56
  180.9 6.0 copy-start.61
  180.9 54.2 %all-to-all-start.3 = ((bf16[1,16,9,4096]{3,2,0,1:T(8,128)(2,1)}), bf16[1,16,9,4096]{3,2,0,1:T(8,128)(2,1)}, u32[]{:S(2)}, u32[]{:S(2)}) async-start(bf16[1,16,9,4096]{3,2,0,1:T(8,128)(2,1)} %bitcast.547), calls=%async_computation.3 | async-start | bytes 4194304 | tf_op jit(solution)/shard_map/all_to_all | solution.py:64
  186.1 301.9 %all-reduce.3.cloned.1.call-start = ((), (), s32[]{:S(2)}) async-start(), calls=%async_computation.4 | async-start | bytes 524288 | tf_op jit(solution)/shard_map/psum | solution.py:94
  262.1 32.8 %collective-permute-start = (bf16[48,4096]{1,0:T(8,128)(2,1)}, bf16[48,4096]{1,0:T(8,128)(2,1)}, u32[]{:S(2)}, u32[]{:S(2)}) collective-permute-start(bf16[48,4096]{1,0:T(8,128)(2,1)} %get-tuple-element.72), channel_id=1, source_target_pairs={{64,0},{128,64},{192,128},{65,1},{129,65},{193,129},{66,2},{130,66... | collective-permute-start | bytes 1179656 | tf_op jit(solution)/shard_map/ppermute | solution.py:10
  296.0 10.3 %copy-start.29 = (f32[48,16]{0,1:T(8,128)S(1)}, f32[48,16]{0,1:T(8,128)}, u32[]{:S(2)}) copy-start(f32[48,16]{0,1:T(8,128)} %copy-done.28) | copy-start | bytes 9220
  307.0 3.8 copy-start.32
  307.0 5.1 copy-start.4
  310.8 13.2 %collective-permute-start.1 = (bf16[48,4096]{1,0:T(8,128)(2,1)}, bf16[48,4096]{1,0:T(8,128)(2,1)}, u32[]{:S(2)}, u32[]{:S(2)}) collective-permute-start(bf16[48,4096]{1,0:T(8,128)(2,1)} %get-tuple-element.76), channel_id=1, source_target_pairs={{64,0},{128,64},{192,128},{65,1},{129,65},{193,129},{66,2},{130,66... | collective-permute-start | bytes 1179656 | tf_op jit(solution)/shard_map/ppermute | solution.py:10
  325.2 10.3 %copy-start.25 = (f32[48,16]{0,1:T(8,128)S(1)}, f32[48,16]{0,1:T(8,128)}, u32[]{:S(2)}) copy-start(f32[48,16]{0,1:T(8,128)} %copy-done.24) | copy-start | bytes 9220
  336.2 3.8 copy-start.34
  336.2 5.1 copy-start.5
  340.0 11.7 %collective-permute-start.2 = (bf16[48,4096]{1,0:T(8,128)(2,1)}, bf16[48,4096]{1,0:T(8,128)(2,1)}, u32[]{:S(2)}, u32[]{:S(2)}) collective-permute-start(bf16[48,4096]{1,0:T(8,128)(2,1)} %get-tuple-element.80), channel_id=1, source_target_pairs={{64,0},{128,64},{192,128},{65,1},{129,65},{193,129},{66,2},{130,66... | collective-permute-start | bytes 1179656 | tf_op jit(solution)/shard_map/ppermute | solution.py:10
  352.8 10.3 %copy-start.27 = (f32[48,16]{0,1:T(8,128)S(1)}, f32[48,16]{0,1:T(8,128)}, u32[]{:S(2)}) copy-start(f32[48,16]{0,1:T(8,128)} %copy-done.26) | copy-start | bytes 9220
  363.8 3.8 copy-start.36
  363.8 5.1 copy-start.6
  367.6 13.3 %collective-permute-start.3 = (bf16[48,4096]{1,0:T(8,128)(2,1)}, bf16[48,4096]{1,0:T(8,128)(2,1)}, u32[]{:S(2)}, u32[]{:S(2)}) collective-permute-start(bf16[48,4096]{1,0:T(8,128)(2,1)} %get-tuple-element.84), channel_id=1, source_target_pairs={{64,0},{128,64},{192,128},{65,1},{129,65},{193,129},{66,2},{130,66... | collective-permute-start | bytes 1179656 | tf_op jit(solution)/shard_map/ppermute | solution.py:10
  384.7 3.7 copy-start.38
  384.8 5.2 copy-start.2
  384.8 5.2 copy-start.12
  384.8 5.2 copy-start.35
  384.8 5.4 copy-start.37
  388.5 12.1 %collective-permute-start.4 = (bf16[48,4096]{1,0:T(8,128)(2,1)S(1)}, bf16[48,4096]{1,0:T(8,128)(2,1)S(1)}, u32[]{:S(2)}, u32[]{:S(2)}) collective-permute-start(bf16[48,4096]{1,0:T(8,128)(2,1)S(1)} %get-tuple-element.88), channel_id=1, source_target_pairs={{64,0},{128,64},{192,128},{65,1},{129,65},{193,129},{66,2},{130,66... | collective-permute-start | bytes 1179656 | tf_op jit(solution)/shard_map/ppermute | solution.py:10
  402.4 10.1 %copy-start.21 = (f32[48,16]{0,1:T(8,128)S(1)}, f32[48,16]{0,1:T(8,128)}, u32[]{:S(2)}) copy-start(f32[48,16]{0,1:T(8,128)} %copy-done.20) | copy-start | bytes 9220
  413.3 4.9 copy-start.3
  413.3 5.0 copy-start.39
  416.9 10.0 %collective-permute-start.5 = (bf16[48,4096]{1,0:T(8,128)(2,1)S(1)}, bf16[48,4096]{1,0:T(8,128)(2,1)S(1)}, u32[]{:S(2)}, u32[]{:S(2)}) collective-permute-start(bf16[48,4096]{1,0:T(8,128)(2,1)S(1)} %get-tuple-element.92), channel_id=1, source_target_pairs={{64,0},{128,64},{192,128},{65,1},{129,65},{193,129},{66,2},{130,66... | collective-permute-start | bytes 1179656 | tf_op jit(solution)/shard_map/ppermute | solution.py:10
  428.8 4.1 copy-start.44
  428.8 10.1 %copy-start.48 = (f32[48]{0:T(128)S(1)}, f32[48]{0:T(128)}, u32[]{:S(2)}) copy-start(f32[48]{0:T(128)} %copy-done.47) | copy-start | bytes 580
  441.5 159.9 %all-reduce.5.cloned.1.call-start = ((), (), s32[]{:S(2)}) async-start(), calls=%async_computation.5 | async-start | bytes 524288 | tf_op jit(solution)/shard_map/psum | solution.py:94
  446.2 41.8 %copy-start.57 = (f32[48]{0:T(128)S(1)}, f32[48]{0:T(128)}, u32[]{:S(2)}) copy-start(f32[48]{0:T(128)} %get-tuple-element.55) | copy-start | bytes 580
  446.2 41.8 %copy-start.58 = (f32[48]{0:T(128)S(1)}, f32[48]{0:T(128)}, u32[]{:S(2)}) copy-start(f32[48]{0:T(128)} %get-tuple-element.56) | copy-start | bytes 580
  (28 other events, 42.2 us)
Sparse Core Ops, SparseCore 0:
  441.6 46.3 all-reduce.2
  490.4 110.9 all-reduce.4
